TPU v7x, 32 devices: a whole 2x2x4 slice. The times are simulated.
32 devices in a mesh: row: 4 (over y, core), col: 8 (over z, x).
Axes of the slice: x: 2, y: 2, z: 4, core: 2. Of those that a mesh axis runs over, the one named last changes fastest.
Arguments:
- spectra: float32 [2, 16, 1024, 512], P(None, None, ('col', 'row')), as said below
- pair_mask: int32 [4, 8], P('row', 'col'), may hold values 0 or 1
- band_range: int32 [2], replicated, may hold values from 0 to 512, as said below
Outputs:
- correlations: bfloat16 [1024, 1024, 201], P('row', 'col')
Inputs may be any that keep to these rules, and one draw needn't show every extreme that they name: `spectra`: every channel's spectrum carries its own amplitude. band_range[0] < band_range[1].
All inputs are finite; a program needn't handle non-finite values. No bound on the sum of `pair_mask` on one device may be relied on, other than what follows from the above.
Results may differ from a plain program's by a relative error of at most 0.0061.
Values may be sent and summed in bfloat16 or wider, within the bound.
No kernel may reach another device: no remote copies, remote signals or barrier semaphores. Data moves between devices by JAX's collectives and lax.ppermute only.
A program may use at most 320 MiB of HBM per device.

v0:
```python
import math
import jax
import jax.numpy as jnp
from jax import lax
from jax.sharding import PartitionSpec as P

W = 16
FB = 512
LAGS = 201
NFFT = 15000
F0 = 60
EPS = 1e-06


def whiten(spectra):
    power_mean = jnp.mean(spectra[0] * spectra[0] + spectra[1] * spectra[1], axis=-1, keepdims=True)
    return (spectra * lax.rsqrt(power_mean + EPS)).astype(jnp.bfloat16)


def make_table(band_range):
    freq_index = jnp.arange(FB, dtype=jnp.int32)
    lag_index = jnp.arange(LAGS, dtype=jnp.int32) - LAGS // 2
    turns = jnp.mod((F0 + freq_index)[:, None] * lag_index[None, :], NFFT)
    theta = turns.astype(jnp.float32) * (2.0 * math.pi / NFFT)
    inband = ((freq_index >= band_range[0]) & (freq_index < band_range[1])).astype(jnp.float32)[
        :, None
    ]
    return jnp.concatenate([inband * jnp.cos(theta), -inband * jnp.sin(theta)], axis=0).astype(
        jnp.bfloat16
    )


def pair_block(row_block, col_block, lag_table):
    real_part = jnp.einsum(
        "wap,wbp->abp", row_block[0], col_block[0], preferred_element_type=jnp.float32
    ) + jnp.einsum("wap,wbp->abp", row_block[1], col_block[1], preferred_element_type=jnp.float32)
    imag_part = jnp.einsum(
        "wap,wbp->abp", row_block[1], col_block[0], preferred_element_type=jnp.float32
    ) - jnp.einsum("wap,wbp->abp", row_block[0], col_block[1], preferred_element_type=jnp.float32)
    cross = jnp.stack([real_part, imag_part], axis=2).astype(jnp.bfloat16)
    height = row_block.shape[2]
    width = col_block.shape[2]
    flat = cross.reshape(height * width, 2 * FB)
    summed = jnp.dot(flat, lag_table, preferred_element_type=jnp.float32)
    return (summed * (1.0 / math.sqrt(W * FB))).astype(jnp.bfloat16).reshape(height, width, LAGS)


def body(spectra, pair_mask, band_range):
    whitened = whiten(spectra)
    col_block = lax.all_gather(whitened, "row", axis=2, tiled=True)
    block_width = col_block.shape[2]
    row_count = lax.axis_size("row")
    blocks_per_row = lax.axis_size("col") // row_count
    row_id = lax.axis_index("row")
    col_id = lax.axis_index("col")
    shard_width = whitened.shape[2]
    windows = whitened.shape[1]
    bins = whitened.shape[3]
    strided = lax.all_gather(whitened, "col", axis=2, tiled=True)
    grouped = strided.reshape(2, windows, row_count, blocks_per_row, shard_width, bins)
    moved = lax.all_to_all(grouped, "row", split_axis=2, concat_axis=4, tiled=True)
    row_block = moved.reshape(2, windows, blocks_per_row * row_count * shard_width, bins)
    lag_table = make_table(band_range)
    request = (pair_mask[0, 0] == 1) & (col_id >= row_id * blocks_per_row)
    height = row_block.shape[2]
    return lax.cond(
        request,
        lambda: pair_block(row_block, col_block, lag_table),
        lambda: jnp.zeros((height, block_width, LAGS), jnp.bfloat16),
    )


def solution(mesh):
    return jax.shard_map(
        body,
        mesh=mesh,
        in_specs=(P(None, None, ("col", "row"), None), P("row", "col"), P()),
        out_specs=P("row", "col", None),
        check_vma=False,
    )
```

profile of v0, /device:TPU:0, one launch (start us, length us, event | category | flops | bytes accessed | tf_op | source)
XLA Modules:
  0.0 639.6 jit_solution(6515462427543158156)
XLA Ops:
  6.5 0.0 all-gather.5.cloned.1.call-start
  6.5 1.7 add_reduce_fusion
  8.3 2.8 multiply_convert_fusion
  11.1 0.0 all-gather.5.cloned.1.call-update
  11.2 0.0 all-gather.3.cloned.1.call-start
  11.2 0.7 all-gather.3.cloned.1.call-update
  11.9 127.0 %all-gather.5.cloned.1.call-done = bf16[2,16,256,512]{3,2,1,0:T(8,128)(2,1)} async-done(((bf16[2,16,32,512]{3,2,1,0:T(8,128)(2,1)}), bf16[2,16,256,512]{3,2,1,0:T(8,128)(2,1)}) %all-gather.5.cloned.1.call-update) | async-done | bytes 8388624 | tf_op jit(solution)/shard_map/all_gather | solution.py:59
  138.9 9.1 %copy.19 = bf16[2,16,4,2,32,512]{5,4,3,1,0,2:T(8,128)(2,1)} copy(bf16[2,16,4,2,32,512]{5,4,3,2,1,0:T(8,128)(2,1)} %bitcast.59) | data formatting | bytes 16777216 | tf_op jit(solution)/shard_map/reshape | solution.py:60
  148.0 0.0 copy-start.1
  148.0 5.8 all-to-all-start
  154.4 0.0 copy-done.1
  154.4 0.6 fusion.22
  155.0 1.1 fusion.20
  156.1 1.1 fusion.19
  157.3 2.6 multiply_convert_fusion.2
  159.9 0.9 pad_maximum_fusion.1
  160.8 27.1 %all-gather.3.cloned.1.call-done = bf16[2,16,128,512]{3,2,1,0:T(8,128)(2,1)} async-done(((bf16[2,16,32,512]{3,2,1,0:T(8,128)(2,1)}), bf16[2,16,128,512]{3,2,1,0:T(8,128)(2,1)}) %all-gather.3.cloned.1.call-update) | async-done | bytes 4194320 | tf_op jit(solution)/shard_map/all_gather | solution.py:50
  187.9 73.7 %all-to-all-done = bf16[2,16,4,2,32,512]{5,4,3,1,0,2:T(8,128)(2,1)} async-done(((bf16[2,16,4,2,32,512]{5,4,3,1,0,2:T(8,128)(2,1)}), bf16[2,16,4,2,32,512]{5,4,3,1,0,2:T(8,128)(2,1)}, u32[]{:S(2)}, u32[]{:S(2)}) %all-to-all-start) | async-done | bytes 8388640 | tf_op jit(solution)/shard_map/all_to_all | solution.py:61
  261.6 371.2 %conditional.1 = (bf16[256,128,201]{1,0,2:T(8,128)(2,1)}) conditional(s32[]{:T(128)} %convert_element_type.30, () %tuple.11, (bf16[2,16,128,512]{3,2,1,0:T(8,128)(2,1)}, bf16[2,16,1,2,4,32,512]{6,5,3,1,0,4,2:T(8,128)(2,1)}, bf16[1024,201]{1,0:T(8,128)(2,1)}) %tuple.12), branch_computations={%region_1.2_spmd, %region_2.3_spmd} | conditional | flops 15750201344 | bytes 807036928 | solution.py:66
  261.6 7.9 %copy.20 = bf16[2,16,128,512]{2,1,3,0:T(8,128)(2,1)} copy(bf16[2,16,128,512]{3,2,1,0:T(8,128)(2,1)} %get-tuple-element.22) | data formatting | bytes 8388608 | tf_op jit(solution)/shard_map
  269.4 6.2 fusion.21
  275.7 7.9 %copy.14 = bf16[16,256,512]{1,0,2:T(8,128)(2,1)} copy(bf16[16,256,512]{2,1,0:T(8,128)(2,1)} %bitcast.57) | data formatting | bytes 8388608 | tf_op jit(solution)/shard_map/cond/branch_1_fun/squeeze | solution.py:35
  283.6 7.8 %copy.15 = bf16[16,256,512]{1,0,2:T(8,128)(2,1)} copy(bf16[16,256,512]{2,1,0:T(8,128)(2,1)} %bitcast.56) | data formatting | bytes 8388608 | tf_op jit(solution)/shard_map/cond/branch_1_fun/squeeze | solution.py:36
  291.4 26.3 %fusion.11 = f32[512,128,256]{2,1,0:T(8,128)} fusion(bf16[16,256,512]{1,0,2:T(8,128)(2,1)} %copy.15, bf16[2,16,128,512]{2,1,3,0:T(8,128)(2,1)} %copy.20), kind=kOutput, calls=%fused_computation.13 | convolution fusion | flops 536870912 | bytes 73400320 | tf_op jit(solution)/shard_map/cond/branch_1_fun/wap,wbp->abp/dot_general | solution.py:37
  317.7 36.4 %fusion.10 = bf16[256,128,1,512]{0,1,3,2:T(8,128)(2,1)} fusion(f32[512,128,256]{2,1,0:T(8,128)} %fusion.11, bf16[16,256,512]{1,0,2:T(8,128)(2,1)} %copy.14, bf16[2,16,128,512]{2,1,3,0:T(8,128)(2,1)} %copy.20), kind=kOutput, calls=%fused_computation.9 | convolution fusion | flops 570425344 | bytes 106954752 | tf_op jit(solution)/shard_map/cond/branch_1_fun/wap,wbp->abp/dot_general | solution.py:39
  354.1 26.3 %fusion.12 = f32[512,128,256]{2,1,0:T(8,128)} fusion(bf16[16,256,512]{1,0,2:T(8,128)(2,1)} %copy.14, bf16[2,16,128,512]{2,1,3,0:T(8,128)(2,1)} %copy.20), kind=kOutput, calls=%fused_computation.14 | convolution fusion | flops 536870912 | bytes 73400320 | tf_op jit(solution)/shard_map/cond/branch_1_fun/wap,wbp->abp/dot_general | solution.py:34
  380.4 36.3 %fusion.9 = bf16[256,128,1,512]{0,1,3,2:T(8,128)(2,1)} fusion(f32[512,128,256]{2,1,0:T(8,128)} %fusion.12, bf16[16,256,512]{1,0,2:T(8,128)(2,1)} %copy.15, bf16[2,16,128,512]{2,1,3,0:T(8,128)(2,1)} %copy.20), kind=kOutput, calls=%fused_computation.8 | convolution fusion | flops 570425344 | bytes 106954752 | tf_op jit(solution)/shard_map/cond/branch_1_fun/wap,wbp->abp/dot_general | solution.py:36
  416.7 44.6 %pad_maximum_fusion = bf16[256,128,2,512]{0,1,3,2:T(8,128)(2,1)} fusion(bf16[256,128,1,512]{0,1,3,2:T(8,128)(2,1)} %fusion.10, bf16[256,128,1,512]{0,1,3,2:T(8,128)(2,1)} %fusion.9), kind=kLoop, calls=%fused_computation.3 | loop fusion | flops 33554432 | bytes 134217728 | tf_op jit(solution)/shard_map/cond/branch_1_fun/stack | solution.py:40
  461.3 0.0 copy-start
  461.3 81.5 %copy.18 = bf16[256,128,2,512]{1,0,3,2:T(8,128)(2,1)} copy(bf16[256,128,2,512]{0,1,3,2:T(8,128)(2,1)} %pad_maximum_fusion) | data formatting | bytes 134217728 | tf_op jit(solution)/shard_map/cond/branch_1_fun/stack | solution.py:40
  542.8 0.0 copy-done
  542.8 75.7 %fusion.6 = bf16[32768,201]{0,1:T(8,128)(2,1)} fusion(bf16[1024,201]{1,0:T(8,128)(2,1)S(1)} %copy-done, bf16[128,8,256,128]{3,2,1,0:T(8,128)(2,1)} %bitcast.19), kind=kOutput, calls=%fused_computation.7 | convolution fusion | flops 13502054400 | bytes 80693248 | tf_op jit(solution)/shard_map/cond/branch_1_fun/dot_general | solution.py:44
  618.5 8.4 %copy.23 = bf16[26,8,256,128]{3,2,1,0:T(8,128)(2,1)S(1)} copy(bf16[26,8,256,128]{3,1,2,0:T(8,128)(2,1)} %bitcast.58) | data formatting | bytes 27262976 | tf_op jit(solution)/shard_map/cond
  626.8 6.0 slice_bitcast_fusion
  (3 shorter events, 0.0 us)
Async XLA Ops:
  6.5 132.4 %all-gather.5.cloned.1.call-start = ((), (), s32[]{:S(2)}) async-start(), calls=%async_computation.2 | async-start | bytes 9437184 | tf_op jit(solution)/shard_map/all_gather | solution.py:59
  11.2 176.7 %all-gather.3.cloned.1.call-start = ((), (), s32[]{:S(2)}) async-start(), calls=%async_computation.1 | async-start | bytes 5242880 | tf_op jit(solution)/shard_map/all_gather | solution.py:50
  148.0 6.4 %copy-start.1 = (s32[2]{0:T(128)S(1)}, s32[2]{0:T(128)}, u32[]{:S(2)}) copy-start(s32[2]{0:T(128)} %param.7) | copy-start | bytes 28
  148.0 113.6 %all-to-all-start = ((bf16[2,16,4,2,32,512]{5,4,3,1,0,2:T(8,128)(2,1)}), bf16[2,16,4,2,32,512]{5,4,3,1,0,2:T(8,128)(2,1)}, u32[]{:S(2)}, u32[]{:S(2)}) async-start(bf16[2,16,4,2,32,512]{5,4,3,1,0,2:T(8,128)(2,1)} %copy.19), calls=%async_computation | async-start | bytes 16777216 | tf_op jit(solution)/shard_map/all_to_all | solution.py:61
  461.3 81.5 %copy-start = (bf16[1024,201]{1,0:T(8,128)(2,1)S(1)}, bf16[1024,201]{1,0:T(8,128)(2,1)}, u32[]{:S(2)}) copy-start(bf16[1024,201]{1,0:T(8,128)(2,1)} %get-tuple-element.17) | copy-start | bytes 1234948 | tf_op jit(solution)/shard_map/cond
Sparse Core Ops, SparseCore 0:
  11.3 127.5 all-gather.4
  140.5 47.3 all-gather.2
where the time goes:
time: 643 us; the launch traced here: 640 us
  waiting for transfers between devices  229 us (36%)
  matrix products  201 us (31%)
  local copies, waits for them, and re-layouts  135 us (21%)
  other arithmetic  55 us (9%)
  between operations  14.1 us (2%)
    all_gather x1, waiting for transfers between devices, body(): strided = lax.all_gather(whitened, 'col', axis=2, tiled=True)  127 us
    another operation x1, local copies, waits for them, and re-layouts, pair_block(): cross = jnp.stack([real_part, imag_part], axis=2).astype(jnp.bfloat16)  81.5 us
    dot_general x1, matrix products, pair_block(): summed = jnp.dot(flat, lag_table, preferred_element_type=jnp.float32)  75.7 us
    all_to_all x1, waiting for transfers between devices, body(): lax.all_to_all(grouped, 'row', split_axis=2, concat_axis=4, tiled=True)  73.7 us
    another operation x1, other arithmetic, pair_block(): cross = jnp.stack([real_part, imag_part], axis=2).astype(jnp.bfloat16)  44.6 us
    dot_general x1, matrix products, pair_block(): jnp.einsum('wap,wbp->abp', row_block[0], col_block[1], preferred_element_...  36.4 us
    dot_general x1, matrix products, pair_block(): jnp.einsum('wap,wbp->abp', row_block[1], col_block[1], preferred_element_...  36.3 us
    all_gather x1, waiting for transfers between devices, body(): col_block = lax.all_gather(whitened, 'row', axis=2, tiled=True)  27.1 us
  transfers between devices with their start and end apart: 3, of which 3 were waited for; matrix products, arithmetic and copies ran while one was open for 2% of the time, Pallas kernels for 0%

commit v1 on v0

--- a/solution.py
+++ b/solution.py
@@ -10,6 +10,19 @@
 NFFT = 15000
 F0 = 60
 EPS = 1e-06
+
+
+def ring_gather(x, axis, dim):
+    size, place, rows = (lax.axis_size(axis), lax.axis_index(axis), x.shape[dim])
+    right = [(i, (i + 1) % size) for i in range(size)]
+    out = jnp.zeros((*x.shape[:dim], size * rows, *x.shape[dim + 1 :]), x.dtype)
+    current = x
+    for step in range(size):
+        holder = (place - step) % size
+        out = lax.dynamic_update_slice_in_dim(out, current, holder * rows, axis=dim)
+        if step < size - 1:
+            current = lax.ppermute(current, axis, right)
+    return out
 
 
 def whiten(spectra):
@@ -56,7 +69,7 @@
     shard_width = whitened.shape[2]
     windows = whitened.shape[1]
     bins = whitened.shape[3]
-    strided = lax.all_gather(whitened, "col", axis=2, tiled=True)
+    strided = ring_gather(whitened, "col", 2)
     grouped = strided.reshape(2, windows, row_count, blocks_per_row, shard_width, bins)
     moved = lax.all_to_all(grouped, "row", split_axis=2, concat_axis=4, tiled=True)
     row_block = moved.reshape(2, windows, blocks_per_row * row_count * shard_width, bins)

time: 643 us -> 686 us (1.067)
  waiting for transfers between devices: 229 us -> 251 us
  local copies, waits for them, and re-layouts: 135 us -> 154 us
    ppermute x0 -> x7, waiting for transfers between devices: none -> 165 us  [ring_gather(): current = lax.ppermute(current, axis, right)]
    all_gather x1 -> x0, waiting for transfers between devices: 127 us -> none  [body(): strided = lax.all_gather(whitened, 'col', axis=2, tiled=True)]
    all_gather x1, waiting for transfers between devices: 27.1 us -> 0.01 us  [body(): col_block = lax.all_gather(whitened, 'row', axis=2, tiled=True)]
    dynamic_update_slice x0 -> x7, local copies, waits for them, and re-layouts: none -> 12.5 us  [ring_gather(): out = lax.dynamic_update_slice_in_dim(out, current, holder * rows, axis=dim)]
    all_to_all x1, waiting for transfers between devices: 73.7 us -> 85.8 us  [body(): lax.all_to_all(grouped, 'row', split_axis=2, concat_axis=4, tiled=True)]
  transfers between devices with their start and end apart: 3 -> 9, of which waited for: 3 -> 8; matrix products, arithmetic and copies ran while one was open for 2% -> 4% of each run, Pallas kernels for 0% -> 0%
where the time goes in v1:
time: 686 us; the launch traced here: 683 us
  waiting for transfers between devices  251 us (37%)
  matrix products  201 us (29%)
  local copies, waits for them, and re-layouts  154 us (22%)
  other arithmetic  53.8 us (8%)
  between operations  14.3 us (2%)
  starting transfers between devices  8.72 us (1%)
    ppermute x7, waiting for transfers between devices, ring_gather(): current = lax.ppermute(current, axis, right)  165 us
    all_to_all x1, waiting for transfers between devices, body(): lax.all_to_all(grouped, 'row', split_axis=2, concat_axis=4, tiled=True)  85.8 us
    another operation x1, local copies, waits for them, and re-layouts, pair_block(): cross = jnp.stack([real_part, imag_part], axis=2).astype(jnp.bfloat16)  81.4 us
    dot_general x1, matrix products, pair_block(): summed = jnp.dot(flat, lag_table, preferred_element_type=jnp.float32)  75.6 us
    another operation x1, other arithmetic, pair_block(): cross = jnp.stack([real_part, imag_part], axis=2).astype(jnp.bfloat16)  44.7 us
    dot_general x1, matrix products, pair_block(): jnp.einsum('wap,wbp->abp', row_block[0], col_block[1], preferred_element_...  36.4 us
    dot_general x1, matrix products, pair_block(): jnp.einsum('wap,wbp->abp', row_block[1], col_block[1], preferred_element_...  36.3 us
    dot_general x1, matrix products, pair_block(): jnp.einsum('wap,wbp->abp', row_block[1], col_block[0], preferred_element_...  26.3 us
  transfers between devices with their start and end apart: 9, of which 8 were waited for; matrix products, arithmetic and copies ran while one was open for 4% of the time, Pallas kernels for 0%

profile of v1, /device:TPU:0, one launch (start us, length us, event | category | flops | bytes accessed | tf_op | source)
XLA Modules:
  0.0 682.6 jit_solution(4785973681941353066)
XLA Ops:
  6.5 0.0 copy-start
  6.5 0.0 all-gather.2.cloned.1.call-start
  6.5 1.9 add_reduce_fusion
  8.5 4.3 broadcast_in_dim.2
  12.8 0.0 copy-done
  12.8 1.2 constant_dynamic-update-slice_fusion.7
  14.0 0.0 copy-start.1
  14.0 2.9 collective-permute-start
  17.0 26.2 %collective-permute-done = bf16[2,16,32,512]{3,2,1,0:T(8,128)(2,1)S(1)} collective-permute-done((bf16[2,16,32,512]{3,2,1,0:T(8,128)(2,1)S(1)}, bf16[2,16,32,512]{3,2,1,0:T(8,128)(2,1)S(1)}, u32[]{:S(2)}, u32[]{:S(2)}) %collective-permute-start) | collective-permute-done | bytes 1048608 | tf_op jit(solution)/shard_map/ppermute | solution.py:24
  43.2 0.0 collective-permute-start.1
  43.2 27.0 %collective-permute-done.1 = bf16[2,16,32,512]{3,2,1,0:T(8,128)(2,1)S(1)} collective-permute-done((bf16[2,16,32,512]{3,2,1,0:T(8,128)(2,1)S(1)}, bf16[2,16,32,512]{3,2,1,0:T(8,128)(2,1)S(1)}, u32[]{:S(2)}, u32[]{:S(2)}) %collective-permute-start.1) | collective-permute-done | bytes 1048608 | tf_op jit(solution)/shard_map/ppermute | solution.py:24
  70.2 0.0 collective-permute-start.2
  70.2 26.1 %collective-permute-done.2 = bf16[2,16,32,512]{3,2,1,0:T(8,128)(2,1)S(1)} collective-permute-done((bf16[2,16,32,512]{3,2,1,0:T(8,128)(2,1)S(1)}, bf16[2,16,32,512]{3,2,1,0:T(8,128)(2,1)S(1)}, u32[]{:S(2)}, u32[]{:S(2)}) %collective-permute-start.2) | collective-permute-done | bytes 1048608 | tf_op jit(solution)/shard_map/ppermute | solution.py:24
  96.3 0.0 copy-start.2
  96.3 1.0 copy-done.2
  97.3 0.0 collective-permute-start.3
  97.3 25.2 %collective-permute-done.3 = bf16[2,16,32,512]{3,2,1,0:T(8,128)(2,1)S(1)} collective-permute-done((bf16[2,16,32,512]{3,2,1,0:T(8,128)(2,1)S(1)}, bf16[2,16,32,512]{3,2,1,0:T(8,128)(2,1)S(1)}, u32[]{:S(2)}, u32[]{:S(2)}) %collective-permute-start.3) | collective-permute-done | bytes 1048608 | tf_op jit(solution)/shard_map/ppermute | solution.py:24
  122.5 0.0 copy-start.3
  122.5 1.0 copy-done.3
  123.5 0.0 collective-permute-start.4
  123.5 24.3 %collective-permute-done.4 = bf16[2,16,32,512]{3,2,1,0:T(8,128)(2,1)S(1)} collective-permute-done((bf16[2,16,32,512]{3,2,1,0:T(8,128)(2,1)S(1)}, bf16[2,16,32,512]{3,2,1,0:T(8,128)(2,1)S(1)}, u32[]{:S(2)}, u32[]{:S(2)}) %collective-permute-start.4) | collective-permute-done | bytes 1048608 | tf_op jit(solution)/shard_map/ppermute | solution.py:24
  147.8 0.0 copy-start.4
  147.8 1.0 copy-done.4
  148.7 0.0 collective-permute-start.5
  148.7 23.5 %collective-permute-done.5 = bf16[2,16,32,512]{3,2,1,0:T(8,128)(2,1)} collective-permute-done((bf16[2,16,32,512]{3,2,1,0:T(8,128)(2,1)S(1)}, bf16[2,16,32,512]{3,2,1,0:T(8,128)(2,1)}, u32[]{:S(2)}, u32[]{:S(2)}) %collective-permute-start.5) | collective-permute-done | bytes 1048608 | tf_op jit(solution)/shard_map/ppermute | solution.py:24
  172.2 0.0 collective-permute-start.6
  172.2 0.0 copy-done.1
  172.2 0.0 all-gather.2.cloned.1.call-update
  172.2 0.0 copy-start.5
  172.4 1.1 constant_dynamic-update-slice_fusion.6
  173.4 1.0 constant_dynamic-update-slice_fusion.5
  174.5 2.3 constant_dynamic-update-slice_fusion.4
  176.8 2.3 constant_dynamic-update-slice_fusion.3
  179.1 0.0 copy-done.5
  179.1 1.0 constant_dynamic-update-slice_fusion.2
  180.1 2.4 constant_dynamic-update-slice_fusion.1
  182.5 12.4 %collective-permute-done.6 = bf16[2,16,32,512]{3,2,1,0:T(8,128)(2,1)} collective-permute-done((bf16[2,16,32,512]{3,2,1,0:T(8,128)(2,1)}, bf16[2,16,32,512]{3,2,1,0:T(8,128)(2,1)}, u32[]{:S(2)}, u32[]{:S(2)}) %collective-permute-start.6) | collective-permute-done | bytes 1048608 | tf_op jit(solution)/shard_map/ppermute | solution.py:24
  194.9 2.3 constant_dynamic-update-slice_fusion
  197.3 8.3 %copy.19 = bf16[2,16,4,2,32,512]{5,4,3,1,0,2:T(8,128)(2,1)} copy(bf16[2,16,4,2,32,512]{5,4,3,2,1,0:T(8,128)(2,1)} %bitcast.9) | data formatting | bytes 16777216 | tf_op jit(solution)/shard_map/reshape | solution.py:73
  205.6 0.0 copy-start.7
  205.6 5.8 all-to-all-start
  212.1 0.0 copy-done.7
  212.1 0.6 fusion.22
  212.7 1.3 fusion.20
  214.0 1.3 fusion.19
  215.3 2.6 multiply_convert_fusion.2
  217.9 0.9 pad_maximum_fusion.1
  218.8 85.8 %all-to-all-done = bf16[2,16,4,2,32,512]{5,4,3,1,0,2:T(8,128)(2,1)} async-done(((bf16[2,16,4,2,32,512]{5,4,3,1,0,2:T(8,128)(2,1)}), bf16[2,16,4,2,32,512]{5,4,3,1,0,2:T(8,128)(2,1)}, u32[]{:S(2)}, u32[]{:S(2)}) %all-to-all-start) | async-done | bytes 8388640 | tf_op jit(solution)/shard_map/all_to_all | solution.py:74
  304.6 371.2 %conditional.1 = (bf16[256,128,201]{1,0,2:T(8,128)(2,1)}) conditional(s32[]{:T(128)} %convert_element_type.30, () %tuple.11, (bf16[2,16,128,512]{3,2,1,0:T(8,128)(2,1)}, bf16[2,16,1,2,4,32,512]{6,5,3,1,0,4,2:T(8,128)(2,1)}, bf16[1024,201]{1,0:T(8,128)(2,1)}) %tuple.12), branch_computations={%region_1.2_spmd, %region_2.3_spmd} | conditional | flops 15750201344 | bytes 807036928 | solution.py:79
  304.6 7.9 %copy.20 = bf16[2,16,128,512]{2,1,3,0:T(8,128)(2,1)} copy(bf16[2,16,128,512]{3,2,1,0:T(8,128)(2,1)} %get-tuple-element.22) | data formatting | bytes 8388608 | tf_op jit(solution)/shard_map
  312.5 6.2 fusion.21
  318.7 7.9 %copy.14 = bf16[16,256,512]{1,0,2:T(8,128)(2,1)} copy(bf16[16,256,512]{2,1,0:T(8,128)(2,1)} %bitcast.57) | data formatting | bytes 8388608 | tf_op jit(solution)/shard_map/cond/branch_1_fun/squeeze | solution.py:48
  326.6 7.8 %copy.15 = bf16[16,256,512]{1,0,2:T(8,128)(2,1)} copy(bf16[16,256,512]{2,1,0:T(8,128)(2,1)} %bitcast.56) | data formatting | bytes 8388608 | tf_op jit(solution)/shard_map/cond/branch_1_fun/squeeze | solution.py:49
  334.5 26.3 %fusion.11 = f32[512,128,256]{2,1,0:T(8,128)} fusion(bf16[16,256,512]{1,0,2:T(8,128)(2,1)} %copy.15, bf16[2,16,128,512]{2,1,3,0:T(8,128)(2,1)} %copy.20), kind=kOutput, calls=%fused_computation.13 | convolution fusion | flops 536870912 | bytes 73400320 | tf_op jit(solution)/shard_map/cond/branch_1_fun/wap,wbp->abp/dot_general | solution.py:50
  360.7 36.4 %fusion.10 = bf16[256,128,1,512]{0,1,3,2:T(8,128)(2,1)} fusion(f32[512,128,256]{2,1,0:T(8,128)} %fusion.11, bf16[16,256,512]{1,0,2:T(8,128)(2,1)} %copy.14, bf16[2,16,128,512]{2,1,3,0:T(8,128)(2,1)} %copy.20), kind=kOutput, calls=%fused_computation.9 | convolution fusion | flops 570425344 | bytes 106954752 | tf_op jit(solution)/shard_map/cond/branch_1_fun/wap,wbp->abp/dot_general | solution.py:52
  397.2 26.3 %fusion.12 = f32[512,128,256]{2,1,0:T(8,128)} fusion(bf16[16,256,512]{1,0,2:T(8,128)(2,1)} %copy.14, bf16[2,16,128,512]{2,1,3,0:T(8,128)(2,1)} %copy.20), kind=kOutput, calls=%fused_computation.14 | convolution fusion | flops 536870912 | bytes 73400320 | tf_op jit(solution)/shard_map/cond/branch_1_fun/wap,wbp->abp/dot_general | solution.py:47
  423.4 36.3 %fusion.9 = bf16[256,128,1,512]{0,1,3,2:T(8,128)(2,1)} fusion(f32[512,128,256]{2,1,0:T(8,128)} %fusion.12, bf16[16,256,512]{1,0,2:T(8,128)(2,1)} %copy.15, bf16[2,16,128,512]{2,1,3,0:T(8,128)(2,1)} %copy.20), kind=kOutput, calls=%fused_computation.8 | convolution fusion | flops 570425344 | bytes 106954752 | tf_op jit(solution)/shard_map/cond/branch_1_fun/wap,wbp->abp/dot_general | solution.py:49
  459.7 44.7 %pad_maximum_fusion = bf16[256,128,2,512]{0,1,3,2:T(8,128)(2,1)} fusion(bf16[256,128,1,512]{0,1,3,2:T(8,128)(2,1)} %fusion.10, bf16[256,128,1,512]{0,1,3,2:T(8,128)(2,1)} %fusion.9), kind=kLoop, calls=%fused_computation.3 | loop fusion | flops 33554432 | bytes 134217728 | tf_op jit(solution)/shard_map/cond/branch_1_fun/stack | solution.py:53
  504.4 0.0 copy-start.6
  504.4 81.4 %copy.18 = bf16[256,128,2,512]{1,0,3,2:T(8,128)(2,1)} copy(bf16[256,128,2,512]{0,1,3,2:T(8,128)(2,1)} %pad_maximum_fusion) | data formatting | bytes 134217728 | tf_op jit(solution)/shard_map/cond/branch_1_fun/stack | solution.py:53
  585.8 0.0 copy-done.6
  585.8 75.6 %fusion.6 = bf16[32768,201]{0,1:T(8,128)(2,1)} fusion(bf16[1024,201]{1,0:T(8,128)(2,1)S(1)} %copy-done.6, bf16[128,8,256,128]{3,2,1,0:T(8,128)(2,1)} %bitcast.19), kind=kOutput, calls=%fused_computation.7 | convolution fusion | flops 13502054400 | bytes 80693248 | tf_op jit(solution)/shard_map/cond/branch_1_fun/dot_general | solution.py:57
  661.5 8.4 %copy.23 = bf16[26,8,256,128]{3,2,1,0:T(8,128)(2,1)S(1)} copy(bf16[26,8,256,128]{3,1,2,0:T(8,128)(2,1)} %bitcast.58) | data formatting | bytes 27262976 | tf_op jit(solution)/shard_map/cond
  669.8 6.0 slice_bitcast_fusion
  (4 shorter events, 0.0 us)
Async XLA Ops:
  6.5 6.3 copy-start
  6.5 212.3 %all-gather.2.cloned.1.call-start = ((), (), s32[]{:S(2)}) async-start(), calls=%async_computation.1 | async-start | bytes 5242880 | tf_op jit(solution)/shard_map/all_gather | solution.py:63
  14.0 158.2 %copy-start.1 = (bf16[2,16,32,512]{3,2,1,0:T(8,128)(2,1)}, bf16[2,16,32,512]{3,2,1,0:T(8,128)(2,1)S(1)}, u32[]{:S(2)}) copy-start(bf16[2,16,32,512]{3,2,1,0:T(8,128)(2,1)S(1)} %get-tuple-element.26) | copy-start | bytes 3145732
  14.0 29.1 %collective-permute-start = (bf16[2,16,32,512]{3,2,1,0:T(8,128)(2,1)S(1)}, bf16[2,16,32,512]{3,2,1,0:T(8,128)(2,1)S(1)}, u32[]{:S(2)}, u32[]{:S(2)}) collective-permute-start(bf16[2,16,32,512]{3,2,1,0:T(8,128)(2,1)S(1)} %get-tuple-element.26), channel_id=1, source_target_pairs={{0,1},{1,2},{2,3},{3,4},{4,5},{5,6},{6,7},{7,0},{8,9},{9,10},{10,1... | collective-permute-start | bytes 3145736 | tf_op jit(solution)/shard_map/ppermute | solution.py:24
  43.2 27.0 %collective-permute-start.1 = (bf16[2,16,32,512]{3,2,1,0:T(8,128)(2,1)S(1)}, bf16[2,16,32,512]{3,2,1,0:T(8,128)(2,1)S(1)}, u32[]{:S(2)}, u32[]{:S(2)}) collective-permute-start(bf16[2,16,32,512]{3,2,1,0:T(8,128)(2,1)S(1)} %collective-permute-done), channel_id=1, source_target_pairs={{0,1},{1,2},{2,3},{3,4},{4,5},{5,6},{6,7},{7,0},{8,9},{9,10},{10,1... | collective-permute-start | bytes 3145736 | tf_op jit(solution)/shard_map/ppermute | solution.py:24
  70.2 26.1 %collective-permute-start.2 = (bf16[2,16,32,512]{3,2,1,0:T(8,128)(2,1)S(1)}, bf16[2,16,32,512]{3,2,1,0:T(8,128)(2,1)S(1)}, u32[]{:S(2)}, u32[]{:S(2)}) collective-permute-start(bf16[2,16,32,512]{3,2,1,0:T(8,128)(2,1)S(1)} %collective-permute-done.1), channel_id=1, source_target_pairs={{0,1},{1,2},{2,3},{3,4},{4,5},{5,6},{6,7},{7,0},{8,9},{9,10},{10,1... | collective-permute-start | bytes 3145736 | tf_op jit(solution)/shard_map/ppermute | solution.py:24
  96.3 1.0 copy-start.2
  97.3 25.2 %collective-permute-start.3 = (bf16[2,16,32,512]{3,2,1,0:T(8,128)(2,1)S(1)}, bf16[2,16,32,512]{3,2,1,0:T(8,128)(2,1)S(1)}, u32[]{:S(2)}, u32[]{:S(2)}) collective-permute-start(bf16[2,16,32,512]{3,2,1,0:T(8,128)(2,1)S(1)} %collective-permute-done.2), channel_id=1, source_target_pairs={{0,1},{1,2},{2,3},{3,4},{4,5},{5,6},{6,7},{7,0},{8,9},{9,10},{10,1... | collective-permute-start | bytes 3145736 | tf_op jit(solution)/shard_map/ppermute | solution.py:24
  122.5 1.0 copy-start.3
  123.5 24.3 %collective-permute-start.4 = (bf16[2,16,32,512]{3,2,1,0:T(8,128)(2,1)S(1)}, bf16[2,16,32,512]{3,2,1,0:T(8,128)(2,1)S(1)}, u32[]{:S(2)}, u32[]{:S(2)}) collective-permute-start(bf16[2,16,32,512]{3,2,1,0:T(8,128)(2,1)S(1)} %collective-permute-done.3), channel_id=1, source_target_pairs={{0,1},{1,2},{2,3},{3,4},{4,5},{5,6},{6,7},{7,0},{8,9},{9,10},{10,1... | collective-permute-start | bytes 3145736 | tf_op jit(solution)/shard_map/ppermute | solution.py:24
  147.8 1.0 copy-start.4
  148.7 23.5 %collective-permute-start.5 = (bf16[2,16,32,512]{3,2,1,0:T(8,128)(2,1)S(1)}, bf16[2,16,32,512]{3,2,1,0:T(8,128)(2,1)}, u32[]{:S(2)}, u32[]{:S(2)}) collective-permute-start(bf16[2,16,32,512]{3,2,1,0:T(8,128)(2,1)S(1)} %collective-permute-done.4), channel_id=1, source_target_pairs={{0,1},{1,2},{2,3},{3,4},{4,5},{5,6},{6,7},{7,0},{8,9},{9,10},{10,1... | collective-permute-start | bytes 3145736 | tf_op jit(solution)/shard_map/ppermute | solution.py:24
  172.2 22.8 %collective-permute-start.6 = (bf16[2,16,32,512]{3,2,1,0:T(8,128)(2,1)}, bf16[2,16,32,512]{3,2,1,0:T(8,128)(2,1)}, u32[]{:S(2)}, u32[]{:S(2)}) collective-permute-start(bf16[2,16,32,512]{3,2,1,0:T(8,128)(2,1)} %collective-permute-done.5), channel_id=1, source_target_pairs={{0,1},{1,2},{2,3},{3,4},{4,5},{5,6},{6,7},{7,0},{8,9},{9,10},{10,1... | collective-permute-start | bytes 3145736 | tf_op jit(solution)/shard_map/ppermute | solution.py:24
  172.2 6.9 %copy-start.5 = (bf16[2,16,32,512]{3,2,1,0:T(8,128)(2,1)S(1)}, bf16[2,16,32,512]{3,2,1,0:T(8,128)(2,1)}, u32[]{:S(2)}) copy-start(bf16[2,16,32,512]{3,2,1,0:T(8,128)(2,1)} %copy-done.4) | copy-start | bytes 3145732
  205.6 6.4 copy-start.7
  205.6 98.9 %all-to-all-start = ((bf16[2,16,4,2,32,512]{5,4,3,1,0,2:T(8,128)(2,1)}), bf16[2,16,4,2,32,512]{5,4,3,1,0,2:T(8,128)(2,1)}, u32[]{:S(2)}, u32[]{:S(2)}) async-start(bf16[2,16,4,2,32,512]{5,4,3,1,0,2:T(8,128)(2,1)} %copy.19), calls=%async_computation | async-start | bytes 16777216 | tf_op jit(solution)/shard_map/all_to_all | solution.py:74
  504.4 81.4 %copy-start.6 = (bf16[1024,201]{1,0:T(8,128)(2,1)S(1)}, bf16[1024,201]{1,0:T(8,128)(2,1)}, u32[]{:S(2)}) copy-start(bf16[1024,201]{1,0:T(8,128)(2,1)} %get-tuple-element.17) | copy-start | bytes 1234948 | tf_op jit(solution)/shard_map/cond
Sparse Core Ops, SparseCore 0:
  172.3 34.9 all-gather.1
